TPU v7x, 32 devices: a whole 2x2x4 slice. The times are simulated.
32 devices in a mesh: group: 2 (over y), blk: 4 (over z), gz: 2 (over x), view: 2 (over core).
Axes of the slice: x: 2, y: 2, z: 4, core: 2. Of those that a mesh axis runs over, the one named last changes fastest.
Arguments:
- estimate: float32 [32, 128, 128], P(('group', 'gz'), 'blk'), parts along dimension 0, may hold values from 0.5 to 2
- view_tiles: bfloat16 [192, 14, 14, 128], P(('group', 'blk', 'gz', 'view')), parts along dimension 0, may hold values from 0.25 to 4
- tile_pairs: int32 [192, 2], P('group'), parts along dimension 0, may hold values from 0 to 31, as said below
- kernel_table: bfloat16 [6, 16, 7, 7, 7], P('view', ('group', 'blk', 'gz')), parts along dimension 1, may hold values from 0.0014953613 to 0.0059814453
- kernel_ids: int32 [64, 6], P('group'), parts along dimension 0, may hold values from 0 to 7
Outputs:
- estimate_out: float32 [32, 128, 128], P(('group', 'gz'), 'blk'), parts along dimension 0
There are 2 independent parts, one for each index of `group`. A program takes and returns all parts, laid end to end along the dimension named above; each array names one. Nothing has to cross between parts.
Inputs may be any that keep to these rules, and one draw needn't show every extreme that they name: Tile t is stored on the device at position t // 6 in the order blk, gz, view. Its block b = tile_pairs[t, 0] lies in that device's sub-slab (b // 16 is its gz index) and its view tile_pairs[t, 1] in that device's half (view // 3 is its view index). No block has two tiles of one view; every block has at least one tile of each half of the views. The tiles of one device go to at most 3 tiles' worth of blocks with the same (b % 16) // 4, and some device reaches 3; the blocks of one sub-slab with the same (b % 16) // 4 have at most 12 tiles of one half of the views, and some reach it.
All inputs are finite; a program needn't handle non-finite values.
Results may differ from a plain program's by a relative error of at most 0.0003.
Values may be sent and summed in bfloat16 or wider, within the bound.
No kernel may reach another device: no remote copies, remote signals or barrier semaphores. Data moves between devices by JAX's collectives and lax.ppermute only.
A program may use at most 64 MiB of HBM per device.

v0:
```python
import jax
import jax.numpy as jnp
from jax import lax
from jax.sharding import PartitionSpec as P

ITERS = 2


def extended_2(array, sides, width):
    for axis, dim in sides:
        peers, length = (lax.axis_size(axis), array.shape[dim])
        up = [(i, (i + 1) % peers) for i in range(peers - 1)]
        down = [(j, i) for i, j in up]
        last = lax.slice_in_dim(array, length - width, length, axis=dim)
        leading = lax.slice_in_dim(array, 0, width, axis=dim)
        before = lax.ppermute(last, axis, up)
        after = lax.ppermute(leading, axis, down)
        array = jnp.concatenate([before, array, after], axis=dim)
    return array


def toeplitz_pair(kernel, cells_x):
    kernel_size = kernel.shape[0]
    kernel_reach = (kernel_size - 1) // 2
    row_index = jnp.arange(cells_x, dtype=jnp.int32)[:, None]
    column_index = jnp.arange(cells_x, dtype=jnp.int32)[None, :]
    tap_index = jnp.arange(kernel_size, dtype=jnp.int32)[:, None, None]
    forward_mask = ((row_index - column_index + kernel_reach)[None] == tap_index).astype(
        jnp.bfloat16
    )
    backward_mask = ((column_index - row_index + kernel_reach)[None] == tap_index).astype(
        jnp.bfloat16
    )
    forward = jnp.einsum(
        "abc,cji->abji", kernel, forward_mask, preferred_element_type=jnp.float32
    ).astype(jnp.bfloat16)
    backward = jnp.einsum(
        "abc,cji->abji", kernel, backward_mask, preferred_element_type=jnp.float32
    ).astype(jnp.bfloat16)
    return (
        forward.reshape(kernel_size, kernel_size * cells_x, cells_x),
        backward.reshape(kernel_size, kernel_size * cells_x, cells_x),
    )


def blurring(extended, forward, extent_z, extent_y):
    kernel_size = forward.shape[0]
    cells_x = extended.shape[2]
    shifted = jnp.stack(
        [extended[:, shift_y : shift_y + extent_y, :] for shift_y in range(kernel_size)], axis=2
    )
    shifted = shifted.reshape(extended.shape[0], extent_y, kernel_size * cells_x)
    accumulated = jnp.zeros((extent_z * extent_y, cells_x), jnp.float32)
    for plane_z in range(kernel_size):
        matrix_rows = shifted[plane_z : plane_z + extent_z].reshape(
            extent_z * extent_y, kernel_size * cells_x
        )
        accumulated = accumulated + jnp.dot(
            matrix_rows, forward[plane_z], preferred_element_type=jnp.float32
        )
    return accumulated.reshape(extent_z, extent_y, cells_x)


def spread(ratio, backward, extent_z, extent_y):
    kernel_size = backward.shape[0]
    kernel_reach = (kernel_size - 1) // 2
    cells_x = ratio.shape[2]
    shifted = jnp.stack(
        [
            ratio[:, 2 * kernel_reach - shift_y : 2 * kernel_reach - shift_y + extent_y, :]
            for shift_y in range(kernel_size)
        ],
        axis=2,
    )
    shifted = shifted.reshape(ratio.shape[0], extent_y, kernel_size * cells_x)
    accumulated = jnp.zeros((extent_z * extent_y, cells_x), jnp.float32)
    for plane_z in range(kernel_size):
        begin_z = 2 * kernel_reach - plane_z
        matrix_rows = shifted[begin_z : begin_z + extent_z].reshape(
            extent_z * extent_y, kernel_size * cells_x
        )
        accumulated = accumulated + jnp.dot(
            matrix_rows, backward[plane_z], preferred_element_type=jnp.float32
        )
    return accumulated.reshape(extent_z, extent_y, cells_x)


def tile_correction(one_tile, extended, kernel, first_z, first_y, volume_z, volume_y):
    extent_z, extent_y, cells_x = one_tile.shape
    kernel_reach = (kernel.shape[0] - 1) // 2
    forward, backward = toeplitz_pair(kernel, cells_x)
    blurred = blurring(extended, forward, extent_z, extent_y)
    cell_z = first_z + jnp.arange(extent_z, dtype=jnp.int32) - kernel_reach
    cell_y = first_y + jnp.arange(extent_y, dtype=jnp.int32) - kernel_reach
    inside = ((cell_z >= 0) & (cell_z < volume_z))[:, None, None] & (
        (cell_y >= 0) & (cell_y < volume_y)
    )[None, :, None]
    ratio = jnp.where(inside, one_tile.astype(jnp.float32) / blurred, 0.0).astype(jnp.bfloat16)
    return spread(ratio, backward, extent_z - 2 * kernel_reach, extent_y - 2 * kernel_reach)


def on_device(estimate, view_tiles, tile_pairs, kernel_table, kernel_ids):
    cells_z, local_y, cells_x = estimate.shape
    tile_count = view_tiles.shape[0]
    extent_y = view_tiles.shape[2]
    views_here = kernel_table.shape[0]
    kernel_reach = (kernel_table.shape[2] - 1) // 2
    block_cells = extent_y - 2 * kernel_reach
    blocks_here = local_y // block_cells
    block_devices = lax.axis_size("blk")
    slab_devices = lax.axis_size("gz")
    core_devices = lax.axis_size("view")
    block_rank = lax.axis_index("blk")
    slab_rank = lax.axis_index("gz")
    core_rank = lax.axis_index("view")
    volume_z = cells_z * slab_devices
    volume_y = local_y * block_devices
    blocks_row = blocks_here * block_devices
    slot_count = (views_here * blocks_here + block_devices - 1) // block_devices
    home_most = views_here * blocks_here
    device_total = block_devices * slab_devices * core_devices
    tile_total = tile_pairs.shape[0]
    kernels = lax.all_gather(kernel_table, ("blk", "gz"), axis=1, tiled=True)
    tile_block = tile_pairs[:, 0]
    tile_view = tile_pairs[:, 1]
    tile_ids = jnp.arange(tile_total, dtype=jnp.int32)
    block_row = tile_block % blocks_row
    home_group = block_row // blocks_here
    home_slab = tile_block // blocks_row
    in_block = block_row % blocks_here
    stored_group = tile_ids // tile_count // (slab_devices * core_devices)
    grouped = home_group.reshape(device_total, tile_count)
    earlier = jnp.arange(tile_count)[:, None] > jnp.arange(tile_count)[None, :]
    slot_rank = jnp.sum(
        ((grouped[:, :, None] == grouped[:, None, :]) & earlier[None]).astype(jnp.int32), axis=2
    ).reshape(-1)
    is_mine = (
        (home_slab == slab_rank)
        & (home_group == block_rank)
        & (tile_view // views_here == core_rank)
    )
    listed = jnp.argsort(jnp.where(is_mine, tile_ids, tile_ids + tile_total))[:home_most]
    live_count = jnp.sum(is_mine.astype(jnp.int32))
    list_source = stored_group[listed]
    list_rank = slot_rank[listed]
    list_block = tile_block[listed]
    list_view = tile_view[listed]
    list_local = in_block[listed]
    first_block = slab_rank * blocks_row + block_rank * blocks_here
    coverage = jnp.sum(
        (tile_block[None, :] == first_block + jnp.arange(blocks_here)[:, None]).astype(jnp.float32),
        axis=1,
    )
    count_field = jnp.repeat(coverage, block_cells)[None, :, None]
    own_ids = (
        block_rank * slab_devices * core_devices + slab_rank * core_devices + core_rank
    ) * tile_count + jnp.arange(tile_count, dtype=jnp.int32)

    def correction_for(one_tile, extended, block_id, view_id):
        kernel = kernels[view_id - core_rank * views_here, kernel_ids[block_id, view_id]]
        first_z = block_id // blocks_row * cells_z
        first_y = block_id % blocks_row * block_cells
        return tile_correction(one_tile, extended, kernel, first_z, first_y, volume_z, volume_y)

    outgoing = jnp.zeros((block_devices, slot_count) + view_tiles.shape[1:], view_tiles.dtype)
    outgoing = outgoing.at[home_group[own_ids], slot_rank[own_ids]].set(view_tiles)
    arrived = lax.all_to_all(outgoing, "blk", split_axis=0, concat_axis=0, tiled=True)
    arrived = arrived.reshape((block_devices * slot_count,) + view_tiles.shape[1:])
    current = estimate
    for iteration in range(ITERS):
        padded = extended_2(current.astype(jnp.bfloat16), (("blk", 1), ("gz", 0)), 2 * kernel_reach)

        def visit_tile(position, summed):
            block_local = list_local[position]
            one_tile = lax.dynamic_index_in_dim(
                arrived, list_source[position] * slot_count + list_rank[position], 0, keepdims=False
            )
            extended = lax.dynamic_slice_in_dim(
                padded, block_local * block_cells, block_cells + 4 * kernel_reach, 1
            )
            correction = correction_for(
                one_tile, extended, list_block[position], list_view[position]
            )
            offset = block_local * block_cells
            window = lax.dynamic_slice_in_dim(summed, offset, block_cells, 1)
            return lax.dynamic_update_slice_in_dim(summed, window + correction, offset, 1)

        summed = lax.fori_loop(0, live_count, visit_tile, jnp.zeros(estimate.shape, jnp.float32))
        combined = lax.psum(summed, "view")
        current = current * combined / count_field
    return current


def solution(mesh):
    in_specs = (
        P(("group", "gz"), "blk", None),
        P(("group", "blk", "gz", "view"), None, None, None),
        P("group", None),
        P("view", ("group", "blk", "gz"), None, None, None),
        P("group", None),
    )
    out_specs = P(("group", "gz"), "blk", None)
    return jax.shard_map(
        on_device, mesh=mesh, in_specs=in_specs, out_specs=out_specs, check_vma=False
    )
```

profile of v0, /device:TPU:0, one launch (start us, length us, event | category | flops | bytes accessed | tf_op | source)
XLA Modules:
  0.0 753.4 jit_solution(275208694247272833)
XLA Ops:
  10.9 2.4 scatter_fusion
  13.2 6.3 all-to-all-start
  19.6 3.9 collective-permute-start
  25.6 2.5 sort.17
  31.3 3.4 collective-permute-start.2
  36.7 36.9 %all_gather.3 = bf16[3,8,7,7,7]{4,3,2,1,0:T(8,128)(2,1)} all-gather(bf16[3,1,7,7,7]{4,3,2,1,0:T(8,128)(2,1)S(1)} %copy-done.4), channel_id=1, replica_groups=mesh['group'=2,'blk'=4,'gz'=2,'view'=2] {'blk','gz'}, dimensions={1}, use_global_device_ids=true | all-gather | bytes 18522 | tf_op jit(solution)/shard_map/all_gather | solution.py:123
  73.7 310.3 %while.26 = (s32[]{:T(128)}, f32[8,32,128]{2,1,0:T(8,128)S(1)}, s32[]{:T(128)}, s32[12]{0:T(128)S(1)}, s32[12]{0:T(128)S(1)}, /*index=5*/s32[12]{0:T(128)S(1)}, ...) while((s32[]{:T(128)}, f32[8,32,128]{2,1,0:T(8,128)S(1)}, ...), condition=%wide.region_5.6_spmd, body=%wide.region_4.5_spmd.sunk | while | flops 442152288 | bytes 46343604 | solution.py:188
  136.8 1.3 convolution_convert_fusion.9
  162.7 1.3 convolution_convert_fusion.9
  188.5 1.3 convolution_convert_fusion.9
  214.3 1.3 convolution_convert_fusion.9
  240.1 1.3 convolution_convert_fusion.9
  265.9 1.3 convolution_convert_fusion.9
  291.7 1.3 convolution_convert_fusion.9
  317.5 1.3 convolution_convert_fusion.9
  343.3 1.3 convolution_convert_fusion.9
  369.1 1.3 convolution_convert_fusion.9
  385.1 17.2 %all-reduce.3.cloned.1.call-done = f32[8,32,128]{2,1,0:T(8,128)} async-done(((f32[8,32,128]{2,1,0:T(8,128)}), f32[8,32,128]{2,1,0:T(8,128)}) %all-reduce.3.cloned.1.call-update) | async-done | bytes 131088 | tf_op jit(solution)/shard_map/psum | solution.py:189
  403.4 3.7 collective-permute-start.4
  408.5 4.2 collective-permute-done.5
  412.8 3.4 collective-permute-start.6
  418.1 4.3 collective-permute-done.7
  422.4 305.3 %while.27 = (s32[]{:T(128)}, f32[8,32,128]{2,1,0:T(8,128)S(1)}, s32[]{:T(128)}, s32[12]{0:T(128)S(1)}, s32[12]{0:T(128)S(1)}, /*index=5*/s32[12]{0:T(128)S(1)}, ...) while((s32[]{:T(128)}, f32[8,32,128]{2,1,0:T(8,128)S(1)}, ...), condition=%wide.region_9.10_spmd, body=%wide.region_8.9_spmd.sunk | while | flops 442152288 | bytes 46343604 | solution.py:188
  430.2 1.4 dynamic_slice.198
  444.9 1.3 convolution_convert_fusion.10
  455.6 1.4 dynamic_slice.198
  470.3 1.3 convolution_convert_fusion.10
  481.0 1.4 dynamic_slice.198
  485.0 1.3 convolution_convert_fusion.11
  506.3 1.4 dynamic_slice.198
  521.0 1.3 convolution_convert_fusion.10
  531.7 1.4 dynamic_slice.198
  535.7 1.3 convolution_convert_fusion.11
  557.1 1.4 dynamic_slice.198
  571.8 1.3 convolution_convert_fusion.10
  582.4 1.4 dynamic_slice.198
  586.5 1.3 convolution_convert_fusion.11
  597.2 1.3 convolution_convert_fusion.10
  607.8 1.4 dynamic_slice.198
  611.8 1.3 convolution_convert_fusion.11
  633.2 1.4 dynamic_slice.198
  647.9 1.3 convolution_convert_fusion.10
  658.6 1.4 dynamic_slice.198
  662.6 1.3 convolution_convert_fusion.11
  683.9 1.4 dynamic_slice.198
  709.3 1.4 dynamic_slice.198
  728.5 16.3 %all-reduce.5.cloned.1.call-done = f32[8,32,128]{2,1,0:T(8,128)} async-done(((f32[8,32,128]{2,1,0:T(8,128)}), f32[8,32,128]{2,1,0:T(8,128)}) %all-reduce.5.cloned.1.call-update) | async-done | bytes 131088 | tf_op jit(solution)/shard_map/psum | solution.py:189
  744.8 1.7 multiply_divide_fusion
  (1953 shorter events, 327.6 us)
Async XLA Ops:
  6.5 4.3 copy-start.3
  9.2 10.3 %copy-start.2 = (f32[8,32,128]{2,1,0:T(8,128)S(1)}, f32[8,32,128]{2,1,0:T(8,128)}, u32[]{:S(2)}) copy-start(f32[8,32,128]{2,1,0:T(8,128)} %param.9) | copy-start | bytes 393220
  13.2 60.5 %all-to-all-start = ((bf16[4,3,14,14,128]{4,3,2,1,0:T(8,128)(2,1)}), bf16[4,3,14,14,128]{4,3,2,1,0:T(8,128)(2,1)}, u32[]{:S(2)}, u32[]{:S(2)}) async-start(bf16[4,3,14,14,128]{4,3,2,1,0:T(8,128)(2,1)} %scatter_fusion), calls=%async_computation | async-start | bytes 1376256 | tf_op jit(solution)/shard_map/all_to_all | solution.py:167
  19.6 17.1 %copy-start.4 = (bf16[3,1,7,7,7]{4,3,2,1,0:T(8,128)(2,1)S(1)}, bf16[3,1,7,7,7]{4,3,2,1,0:T(8,128)(2,1)}, u32[]{:S(2)}) copy-start(bf16[3,1,7,7,7]{4,3,2,1,0:T(8,128)(2,1)} %param.12) | copy-start | bytes 6178
  19.6 382.8 %all-reduce.3.cloned.1.call-start = ((), (), s32[]{:S(2)}) async-start(), calls=%async_computation.1 | async-start | bytes 262144 | tf_op jit(solution)/shard_map/psum | solution.py:189
  19.6 11.6 %collective-permute-start = (bf16[8,6,128]{2,1,0:T(8,128)(2,1)S(1)}, bf16[8,6,128]{2,1,0:T(8,128)(2,1)S(1)}, u32[]{:S(2)}, u32[]{:S(2)}) collective-permute-start(bf16[8,6,128]{2,1,0:T(8,128)(2,1)S(1)} %get-tuple-element.543), channel_id=1, source_target_pairs={{0,4},{4,8},{8,12},{1,5},{5,9},{9,13},{2,6},{6,10},{10,14},{3,7},{... | collective-permute-start | bytes 36872 | tf_op jit(solution)/shard_map/ppermute | solution.py:16
  23.6 7.6 %collective-permute-start.1 = (bf16[8,6,128]{2,1,0:T(8,128)(2,1)S(1)}, bf16[8,6,128]{2,1,0:T(8,128)(2,1)S(1)}, u32[]{:S(2)}, u32[]{:S(2)}) collective-permute-start(bf16[8,6,128]{2,1,0:T(8,128)(2,1)S(1)} %get-tuple-element.544), channel_id=1, source_target_pairs={{4,0},{8,4},{12,8},{5,1},{9,5},{13,9},{6,2},{10,6},{14,10},{7,3},{... | collective-permute-start | bytes 36872 | tf_op jit(solution)/shard_map/ppermute | solution.py:17
  31.3 42.4 %collective-permute-start.2 = (bf16[6,44,128]{2,1,0:T(8,128)(2,1)S(1)}, bf16[6,44,128]{2,1,0:T(8,128)(2,1)S(1)}, u32[]{:S(2)}, u32[]{:S(2)}) collective-permute-start(bf16[6,44,128]{2,1,0:T(8,128)(2,1)S(1)} %get-tuple-element.539), channel_id=1, source_target_pairs={{0,2},{1,3},{4,6},{5,7},{8,10},{9,11},{12,14},{13,15},{16,18},{17,... | collective-permute-start | bytes 202760 | tf_op jit(solution)/shard_map/ppermute | solution.py:16
  34.7 38.9 %collective-permute-start.3 = (bf16[6,44,128]{2,1,0:T(8,128)(2,1)S(1)}, bf16[6,44,128]{2,1,0:T(8,128)(2,1)S(1)}, u32[]{:S(2)}, u32[]{:S(2)}) collective-permute-start(bf16[6,44,128]{2,1,0:T(8,128)(2,1)S(1)} %get-tuple-element.540), channel_id=1, source_target_pairs={{2,0},{3,1},{6,4},{7,5},{10,8},{11,9},{14,12},{15,13},{18,16},{19,... | collective-permute-start | bytes 202760 | tf_op jit(solution)/shard_map/ppermute | solution.py:17
  384.0 0.7 copy-start.1
  384.7 360.1 %all-reduce.5.cloned.1.call-start = ((), (), s32[]{:S(2)}) async-start(), calls=%async_computation.2 | async-start | bytes 262144 | tf_op jit(solution)/shard_map/psum | solution.py:189
  403.4 5.1 collective-permute-start.4
  407.1 5.6 collective-permute-start.5
  412.8 5.3 collective-permute-start.6
  416.1 6.2 collective-permute-start.7
  727.8 0.7 copy-start
Sparse Core Ops, SparseCore 0:
  384.8 17.4 all-reduce.2
  728.6 16.1 all-reduce.4
where the time goes:
time: 762 us; the launch traced here: 753 us
  loops' own time  261 us (34%)
  local copies, waits for them, and re-layouts  202 us (27%)
  matrix products  138 us (18%)
  waiting for transfers between devices  43.3 us (6%)
  blocking collectives  36.9 us (5%)
  other arithmetic  31.9 us (4%)
  starting transfers between devices  26 us (3%)
  between operations  13.7 us (2%)
    another operation x2, loops' own time, on_device(): lax.fori_loop(0, live_count, visit_tile, jnp.zeros(estimate.shape, jnp.fl...  261 us
    dot_general x168, matrix products, blurring(): jnp.dot(matrix_rows, forward[plane_z], preferred_element_type=jnp.float32)  44.2 us
    all_gather x1, blocking collectives, on_device(): kernels = lax.all_gather(kernel_table, ('blk', 'gz'), axis=1, tiled=True)  36.9 us
    slice x192, local copies, waits for them, and re-layouts, blurring(): shifted[plane_z:plane_z + extent_z]  35.4 us
    psum x2, waiting for transfers between devices, on_device(): combined = lax.psum(summed, 'view')  33.6 us
    dot_general x24, matrix products, toeplitz_pair(): jnp.einsum('abc,cji->abji', kernel, forward_mask, preferred_element_type=...  32.2 us
    dot_general x24, matrix products, toeplitz_pair(): jnp.einsum('abc,cji->abji', kernel, backward_mask, preferred_element_type...  32.2 us
    while x624, local copies, waits for them, and re-layouts  32.1 us
  transfers between devices with their start and end apart: 11, of which 7 were waited for; matrix products, arithmetic and copies ran while one was open for 1% of the time, Pallas kernels for 0%

commit v1 on v0

--- a/solution.py
+++ b/solution.py
@@ -186,7 +186,7 @@
             return lax.dynamic_update_slice_in_dim(summed, window + correction, offset, 1)
 
         summed = lax.fori_loop(0, live_count, visit_tile, jnp.zeros(estimate.shape, jnp.float32))
-        combined = lax.psum(summed, "view")
+        combined = jnp.sum(lax.all_gather(summed, "view"), axis=0)
         current = current * combined / count_field
     return current
 

time: 762 us -> 721 us (0.946)
  waiting for transfers between devices: 43.3 us -> 9.29 us
  between operations: 13.7 us -> 0.28 us
  loops' own time: 261 us -> 269 us
    psum x2 -> x0, waiting for transfers between devices: 33.6 us -> none  [on_device(): combined = lax.psum(summed, 'view')]
    another operation x2, loops' own time: 261 us -> 269 us  [on_device(): lax.fori_loop(0, live_count, visit_tile, jnp.zeros(estimate.shape, jnp.fl...]
  transfers between devices with their start and end apart: 11 -> 9, of which waited for: 7 -> 4; matrix products, arithmetic and copies ran while one was open for 1% -> 1% of each run, Pallas kernels for 0% -> 0%
where the time goes in v1:
time: 721 us; the launch traced here: 712 us
  loops' own time  269 us (37%)
  local copies, waits for them, and re-layouts  201 us (28%)
  matrix products  139 us (19%)
  blocking collectives  40.7 us (6%)
  other arithmetic  30.9 us (4%)
  starting transfers between devices  21.4 us (3%)
  waiting for transfers between devices  9.29 us (1%)
    another operation x2, loops' own time, on_device(): lax.fori_loop(0, live_count, visit_tile, jnp.zeros(estimate.shape, jnp.fl...  269 us
    dot_general x168, matrix products, blurring(): jnp.dot(matrix_rows, forward[plane_z], preferred_element_type=jnp.float32)  44.3 us
    all_gather x1, blocking collectives, on_device(): kernels = lax.all_gather(kernel_table, ('blk', 'gz'), axis=1, tiled=True)  36.7 us
    slice x192, local copies, waits for them, and re-layouts, blurring(): shifted[plane_z:plane_z + extent_z]  35.4 us
    dot_general x24, matrix products, toeplitz_pair(): jnp.einsum('abc,cji->abji', kernel, backward_mask, preferred_element_type...  32.2 us
    dot_general x24, matrix products, toeplitz_pair(): jnp.einsum('abc,cji->abji', kernel, forward_mask, preferred_element_type=...  32.2 us
    while x624, local copies, waits for them, and re-layouts  32.1 us
    dynamic_slice x24, local copies, waits for them, and re-layouts, correction_for(): kernel_ids[block_id, view_id]  30.6 us
  transfers between devices with their start and end apart: 9, of which 4 were waited for; matrix products, arithmetic and copies ran while one was open for 1% of the time, Pallas kernels for 0%

profile of v1, /device:TPU:0, one launch (start us, length us, event | category | flops | bytes accessed | tf_op | source)
XLA Modules:
  0.0 711.5 jit_solution(10762943060918239111)
XLA Ops:
  4.3 2.4 scatter_fusion
  6.7 6.4 all-to-all-start
  13.1 3.9 collective-permute-start
  18.3 2.5 sort.17
  25.0 3.4 collective-permute-start.2
  30.0 36.7 %all_gather.15 = bf16[3,8,7,7,7]{4,3,2,1,0:T(8,128)(2,1)} all-gather(bf16[3,1,7,7,7]{4,3,2,1,0:T(8,128)(2,1)S(1)} %copy-done.3), channel_id=1, replica_groups=mesh['group'=2,'blk'=4,'gz'=2,'view'=2] {'blk','gz'}, dimensions={1}, use_global_device_ids=true | all-gather | bytes 18522 | tf_op jit(solution)/shard_map/all_gather | solution.py:123
  66.8 311.2 %while.26 = (s32[]{:T(128)}, f32[8,32,128]{2,1,0:T(8,128)S(1)}, s32[]{:T(128)}, s32[12]{0:T(128)S(1)}, s32[12]{0:T(128)S(1)}, /*index=5*/s32[12]{0:T(128)S(1)}, ...) while((s32[]{:T(128)}, f32[8,32,128]{2,1,0:T(8,128)S(1)}, ...), condition=%wide.region_5.6_spmd, body=%wide.region_4.5_spmd.sunk | while | flops 442152288 | bytes 46343604 | solution.py:188
  78.1 1.3 convolution_convert_fusion.9
  89.6 1.3 convolution_convert_fusion.8
  104.0 1.3 convolution_convert_fusion.9
  115.5 1.3 convolution_convert_fusion.8
  141.4 1.3 convolution_convert_fusion.8
  155.8 1.3 convolution_convert_fusion.9
  167.3 1.3 convolution_convert_fusion.8
  193.1 1.3 convolution_convert_fusion.8
  207.5 1.3 convolution_convert_fusion.9
  219.0 1.3 convolution_convert_fusion.8
  244.9 1.3 convolution_convert_fusion.8
  259.3 1.3 convolution_convert_fusion.9
  270.8 1.3 convolution_convert_fusion.8
  296.7 1.3 convolution_convert_fusion.8
  311.1 1.3 convolution_convert_fusion.9
  322.6 1.3 convolution_convert_fusion.8
  348.4 1.3 convolution_convert_fusion.8
  362.8 1.3 convolution_convert_fusion.9
  374.3 1.3 convolution_convert_fusion.8
  378.0 2.0 all-gather
  382.9 4.2 collective-permute-done.5
  390.4 4.3 collective-permute-done.7
  394.8 313.1 %while.27 = (s32[]{:T(128)}, f32[8,32,128]{2,1,0:T(8,128)S(1)}, s32[]{:T(128)}, s32[12]{0:T(128)S(1)}, s32[12]{0:T(128)S(1)}, /*index=5*/s32[12]{0:T(128)S(1)}, ...) while((s32[]{:T(128)}, f32[8,32,128]{2,1,0:T(8,128)S(1)}, ...), condition=%wide.region_9.10_spmd, body=%wide.region_8.9_spmd.sunk | while | flops 442152288 | bytes 46343604 | solution.py:188
  406.4 1.3 convolution_convert_fusion.11
  417.9 1.3 convolution_convert_fusion.10
  443.9 1.3 convolution_convert_fusion.10
  469.9 1.3 convolution_convert_fusion.10
  496.0 1.3 convolution_convert_fusion.10
  510.5 1.3 convolution_convert_fusion.11
  522.0 1.3 convolution_convert_fusion.10
  548.0 1.3 convolution_convert_fusion.10
  562.5 1.3 convolution_convert_fusion.11
  574.0 1.3 convolution_convert_fusion.10
  600.1 1.3 convolution_convert_fusion.10
  626.1 1.3 convolution_convert_fusion.10
  640.6 1.3 convolution_convert_fusion.11
  652.1 1.3 convolution_convert_fusion.10
  678.1 1.3 convolution_convert_fusion.10
  704.1 1.3 convolution_convert_fusion.10
  707.8 2.0 all-gather.1
  709.9 1.7 multiply_divide_fusion
  (1949 shorter events, 325.7 us)
Async XLA Ops:
  0.0 4.3 copy-start.2
  2.7 10.3 %copy-start = (f32[8,32,128]{2,1,0:T(8,128)S(1)}, f32[8,32,128]{2,1,0:T(8,128)}, u32[]{:S(2)}) copy-start(f32[8,32,128]{2,1,0:T(8,128)} %param.9) | copy-start | bytes 393220
  6.7 60.1 %all-to-all-start = ((bf16[4,3,14,14,128]{4,3,2,1,0:T(8,128)(2,1)}), bf16[4,3,14,14,128]{4,3,2,1,0:T(8,128)(2,1)}, u32[]{:S(2)}, u32[]{:S(2)}) async-start(bf16[4,3,14,14,128]{4,3,2,1,0:T(8,128)(2,1)} %scatter_fusion), calls=%async_computation | async-start | bytes 1376256 | tf_op jit(solution)/shard_map/all_to_all | solution.py:167
  13.0 17.0 %copy-start.3 = (bf16[3,1,7,7,7]{4,3,2,1,0:T(8,128)(2,1)S(1)}, bf16[3,1,7,7,7]{4,3,2,1,0:T(8,128)(2,1)}, u32[]{:S(2)}) copy-start(bf16[3,1,7,7,7]{4,3,2,1,0:T(8,128)(2,1)} %param.12) | copy-start | bytes 6178
  13.1 11.8 %collective-permute-start = (bf16[8,6,128]{2,1,0:T(8,128)(2,1)S(1)}, bf16[8,6,128]{2,1,0:T(8,128)(2,1)S(1)}, u32[]{:S(2)}, u32[]{:S(2)}) collective-permute-start(bf16[8,6,128]{2,1,0:T(8,128)(2,1)S(1)} %get-tuple-element.543), channel_id=1, source_target_pairs={{0,4},{4,8},{8,12},{1,5},{5,9},{9,13},{2,6},{6,10},{10,14},{3,7},{... | collective-permute-start | bytes 36872 | tf_op jit(solution)/shard_map/ppermute | solution.py:16
  17.0 7.9 %collective-permute-start.1 = (bf16[8,6,128]{2,1,0:T(8,128)(2,1)S(1)}, bf16[8,6,128]{2,1,0:T(8,128)(2,1)S(1)}, u32[]{:S(2)}, u32[]{:S(2)}) collective-permute-start(bf16[8,6,128]{2,1,0:T(8,128)(2,1)S(1)} %get-tuple-element.544), channel_id=1, source_target_pairs={{4,0},{8,4},{12,8},{5,1},{9,5},{13,9},{6,2},{10,6},{14,10},{7,3},{... | collective-permute-start | bytes 36872 | tf_op jit(solution)/shard_map/ppermute | solution.py:17
  25.0 41.8 %collective-permute-start.2 = (bf16[6,44,128]{2,1,0:T(8,128)(2,1)S(1)}, bf16[6,44,128]{2,1,0:T(8,128)(2,1)S(1)}, u32[]{:S(2)}, u32[]{:S(2)}) collective-permute-start(bf16[6,44,128]{2,1,0:T(8,128)(2,1)S(1)} %get-tuple-element.539), channel_id=1, source_target_pairs={{0,2},{1,3},{4,6},{5,7},{8,10},{9,11},{12,14},{13,15},{16,18},{17,... | collective-permute-start | bytes 202760 | tf_op jit(solution)/shard_map/ppermute | solution.py:16
  28.4 38.3 %collective-permute-start.3 = (bf16[6,44,128]{2,1,0:T(8,128)(2,1)S(1)}, bf16[6,44,128]{2,1,0:T(8,128)(2,1)S(1)}, u32[]{:S(2)}, u32[]{:S(2)}) collective-permute-start(bf16[6,44,128]{2,1,0:T(8,128)(2,1)S(1)} %get-tuple-element.540), channel_id=1, source_target_pairs={{2,0},{3,1},{6,4},{7,5},{10,8},{11,9},{14,12},{15,13},{18,16},{19,... | collective-permute-start | bytes 202760 | tf_op jit(solution)/shard_map/ppermute | solution.py:17
  380.0 14.7 %copy-start.1 = (f32[8,32,128]{2,1,0:T(8,128)}, f32[8,32,128]{2,1,0:T(8,128)S(1)}, u32[]{:S(2)}) copy-start(f32[8,32,128]{2,1,0:T(8,128)S(1)} %reduce_sum.47) | copy-start | bytes 393220
  380.2 2.7 collective-permute-start.4
  381.5 5.6 collective-permute-start.5
  387.2 3.3 collective-permute-start.6
  388.5 6.2 collective-permute-start.7
